TPU v7x, 512 devices: a whole 4x8x8 slice. The times are simulated.
512 devices in a mesh: gs: 128 (over y, z, core), view: 4 (over x).
Axes of the slice: x: 4, y: 8, z: 8, core: 2. Of those that a mesh axis runs over, the one named last changes fastest.
Arguments:
- features: bfloat16 [131072, 128], P('gs'), may hold values from -6 to 6
- geometry: float32 [4, 9, 131072], P('view', None, 'gs'), as said below
- decoder: bfloat16 [128, 512], replicated, may hold values from -0.5 to 0.5
- teacher: bfloat16 [4, 131072, 512], P('view', 'gs'), may hold values from -3 to 3
- images: float32 [4, 3, 131072], P('view', None, 'gs'), may hold values from 0 to 1
- send_index: int32 [4, 128, 1024], P('view', 'gs'), may hold values from 0 to 1023, as said below
- tile_lists: int32 [4, 512, 8], P('view', 'gs'), may hold values from 0 to 7, as said below
- tile_lengths: int32 [4, 512], P('view', 'gs'), may hold values from 2 to 8
Outputs:
- feature_grad: float32 [131072, 128], P(('gs', 'view'))
- geometry_grad: float32 [4, 9, 131072], P('view', None, 'gs')
- decoder_grad: float32 [128, 512], replicated
Inputs may be any that keep to these rules, and one draw needn't show every extreme that they name: `send_index`: each row (one view, one source device) is a permutation of 0 .. 1023; positions k * 8 to (k + 1) * 8 - 1 hold the Gaussians sent to the device of gs index k. `tile_lists`: the 8 entries of a row are distinct. `geometry`: opacity logits lie in -7.5 .. -4, log conics between -2 log 16 and -2 log 16 + 2 log 4, shears in -2 .. 2, colors in 0 .. 1.
All inputs are finite; a program needn't handle non-finite values.
Results may differ from a plain program's by a relative error of at most 0.0017.
Values may be sent and summed in bfloat16 or wider, within the bound.
A program may use at most 64 MiB of HBM per device.

v0:
```python
import math
import jax
import jax.numpy as jnp
from jax import lax
from jax.sharding import PartitionSpec as P

FEAT = 128
CT = 512
TS = 16
BLK = 128
LIST = 8


def composite(tile_geo, alive_mask, pixel_x, pixel_y):
    delta_x = pixel_x[:, None] - tile_geo[0][None, :]
    delta_y = pixel_y[:, None] - tile_geo[1][None, :]
    conic_a = jnp.exp(tile_geo[2])
    conic_c = jnp.exp(tile_geo[3])
    conic_b = 0.8 * jnp.tanh(tile_geo[4]) * jnp.exp(0.5 * (tile_geo[2] + tile_geo[3]))
    exponent = -0.5 * (
        conic_a * delta_x * delta_x
        + 2.0 * conic_b * delta_x * delta_y
        + conic_c * delta_y * delta_y
    )
    opacity = alive_mask * jax.nn.sigmoid(tile_geo[5])
    alpha_val = opacity[None, :] * jnp.exp(exponent)
    log_keep = jnp.log1p(-alpha_val)
    pixel_count = pixel_x.shape[0]
    blocked = log_keep.reshape(pixel_count, LIST, BLK)
    inner = jnp.cumsum(blocked, axis=2) - blocked
    block_sums = jnp.sum(blocked, axis=2)
    outer = jnp.cumsum(block_sums, axis=1) - block_sums
    before = (inner + outer[:, :, None]).reshape(pixel_count, LIST * BLK)
    weights = alpha_val * jnp.exp(before)
    pixel_color = jnp.einsum("pi,ci->cp", weights, tile_geo[6:9], precision=lax.Precision.HIGHEST)
    return (weights, pixel_color)


def device_terms(
    recv_geo, recv_feat, decoder, teacher_dev, images_dev, lists, lengths, shard_index
):
    nblocks = recv_feat.shape[0] // BLK
    tile_pixels = TS * TS
    geo_blocks = recv_geo.reshape(9, nblocks, BLK)
    feat_blocks = recv_feat.reshape(nblocks, BLK, FEAT)
    within = jnp.arange(tile_pixels, dtype=jnp.int32)
    block_range = jnp.arange(nblocks, dtype=jnp.int32)
    slot_range = jnp.arange(LIST, dtype=jnp.int32)

    def tile_step(totals, tile_index):
        decoder_sum, geo_acc, feat_acc = totals
        block_ids = lists[tile_index]
        count = lengths[tile_index]
        alive_mask = jnp.broadcast_to(
            (slot_range < count).astype(jnp.float32)[:, None], (LIST, BLK)
        ).reshape(LIST * BLK)
        tile_geo = jnp.take(geo_blocks, block_ids, axis=1).reshape(9, LIST * BLK)
        feat_tile = jnp.take(feat_blocks, block_ids, axis=0).reshape(LIST * BLK, FEAT)
        column = 2 * TS * (shard_index % 30) + TS * (tile_index % 2) + within % TS
        row_index = 2 * TS * (shard_index // 30) + TS * (tile_index // 2) + within // TS
        pixel_x = column.astype(jnp.float32) + 0.5
        pixel_y = row_index.astype(jnp.float32) + 0.5
        (weights, pixel_color), pullback = jax.vjp(
            lambda geo_part: composite(geo_part, alive_mask, pixel_x, pixel_y), tile_geo
        )
        weight_b = weights.astype(jnp.bfloat16)
        rendered = jnp.dot(weight_b, feat_tile, preferred_element_type=jnp.float32).astype(
            jnp.bfloat16
        )
        pred = jnp.dot(rendered, decoder, preferred_element_type=jnp.float32)
        teacher_rows = lax.dynamic_slice_in_dim(
            teacher_dev, tile_index * tile_pixels, tile_pixels, 0
        )
        error_feat = pred - teacher_rows.astype(jnp.float32)
        gpred = (error_feat / jnp.sqrt(error_feat * error_feat + 0.04)).astype(jnp.bfloat16)
        grender = lax.dot_general(
            gpred, decoder, (((1,), (1,)), ((), ())), preferred_element_type=jnp.float32
        ).astype(jnp.bfloat16)
        decoder_sum = decoder_sum + lax.dot_general(
            rendered, gpred, (((0,), (0,)), ((), ())), preferred_element_type=jnp.float32
        )
        image_cols = lax.dynamic_slice_in_dim(images_dev, tile_index * tile_pixels, tile_pixels, 1)
        error_color = pixel_color - image_cols
        gcolor = error_color / jnp.sqrt(error_color * error_color + 0.04)
        gweight = lax.dot_general(
            grender, feat_tile, (((1,), (1,)), ((), ())), preferred_element_type=jnp.float32
        )
        gfeat_tile = lax.dot_general(
            weight_b, grender, (((0,), (0,)), ((), ())), preferred_element_type=jnp.float32
        )
        (ggeo_tile,) = pullback((gweight, gcolor))
        hits = (block_ids[:, None] == block_range[None, :]).astype(jnp.float32)
        geo_acc = geo_acc + jnp.einsum(
            "clb,ln->cnb", ggeo_tile.reshape(9, LIST, BLK), hits, precision=lax.Precision.HIGHEST
        )
        feat_acc = feat_acc + jnp.einsum(
            "ln,lbf->nbf",
            hits,
            gfeat_tile.reshape(LIST, BLK, FEAT),
            precision=lax.Precision.HIGHEST,
        )
        return ((decoder_sum, geo_acc, feat_acc), None)

    start_totals = (
        jnp.zeros((FEAT, CT), jnp.float32),
        jnp.zeros((9, nblocks, BLK), jnp.float32),
        jnp.zeros((nblocks, BLK, FEAT), jnp.float32),
    )
    tile_range = jnp.arange(lists.shape[0], dtype=jnp.int32)
    (decoder_sum, geo_acc, feat_acc), _ = lax.scan(tile_step, start_totals, tile_range)
    return (decoder_sum, geo_acc.reshape(9, nblocks * BLK), feat_acc.reshape(nblocks * BLK, FEAT))


def on_device(features, geometry, decoder, teacher, images, send_index, tile_lists, tile_lengths):
    send_order = send_index[0, 0]
    shard_index = lax.axis_index("gs")
    geo_send = jnp.take(geometry[0], send_order, axis=1)
    recv_geo = lax.all_to_all(geo_send, "gs", split_axis=1, concat_axis=1, tiled=True)
    feat_send = jnp.take(features, send_order, axis=0)
    recv_feat = lax.all_to_all(feat_send, "gs", split_axis=0, concat_axis=0, tiled=True)
    decoder_sum, geo_acc, feat_acc = device_terms(
        recv_geo,
        recv_feat,
        decoder,
        teacher[0],
        images[0],
        tile_lists[0],
        tile_lengths[0],
        shard_index,
    )
    returned_geo = lax.all_to_all(geo_acc, "gs", split_axis=1, concat_axis=1, tiled=True)
    returned_feat = lax.all_to_all(feat_acc, "gs", split_axis=0, concat_axis=0, tiled=True)
    geo_own = jnp.zeros_like(returned_geo).at[:, send_order].set(returned_geo)
    feat_own = jnp.zeros_like(returned_feat).at[send_order].set(returned_feat)
    quarter = feat_own.shape[0] // lax.axis_size("view")
    summed = lax.psum(feat_own, "view")
    feature_grad = lax.dynamic_slice_in_dim(summed, lax.axis_index("view") * quarter, quarter, 0)
    pixel_total = lax.axis_size("gs") * lax.axis_size("view") * tile_lists.shape[1] * TS * TS
    decoder_grad = lax.psum(decoder_sum, ("gs", "view")) * (1.0 / math.sqrt(pixel_total))
    return (feature_grad, geo_own[None], decoder_grad)


def solution(mesh):
    placed = (
        P("gs", None),
        P("view", None, "gs"),
        P(),
        P("view", "gs", None),
        P("view", None, "gs"),
        P("view", "gs", None),
        P("view", "gs", None),
        P("view", "gs"),
    )
    return jax.shard_map(
        on_device,
        mesh=mesh,
        in_specs=placed,
        out_specs=(P(("gs", "view"), None), P("view", None, "gs"), P()),
        check_vma=False,
    )
```

profile of v0, /device:TPU:8, one launch (start us, length us, event | category | flops | bytes accessed | tf_op | source)
XLA Modules:
  0.0 610.4 jit_solution(10011325874883574381)
XLA Ops:
  10.2 2.8 gather_fusion.2
  14.1 17.4 %all-to-all-start = ((f32[9,128,8]{0,2,1:T(8,128)}), f32[9,128,8]{0,2,1:T(8,128)S(1)}, u32[]{:S(2)}, u32[]{:S(2)}) async-start(f32[9,128,8]{0,2,1:T(8,128)} %bitcast_select_fusion.1), calls=%async_computation | async-start | bytes 1048576 | tf_op jit(solution)/shard_map/all_to_all | solution.py:118
  31.5 3.2 gather_fusion.3
  35.6 16.2 %all-to-all-done = f32[9,128,8]{0,2,1:T(8,128)S(1)} async-done(((f32[9,128,8]{0,2,1:T(8,128)}), f32[9,128,8]{0,2,1:T(8,128)S(1)}, u32[]{:S(2)}, u32[]{:S(2)}) %all-to-all-start) | async-done | bytes 36896 | tf_op jit(solution)/shard_map/all_to_all | solution.py:118
  51.8 6.5 %all-to-all-start.1 = ((bf16[128,8,128]{2,1,0:T(8,128)(2,1)}), bf16[128,8,128]{2,1,0:T(8,128)(2,1)S(1)}, u32[]{:S(2)}, u32[]{:S(2)}) async-start(bf16[128,8,128]{2,1,0:T(8,128)(2,1)} %bitcast_select_fusion.2), calls=%async_computation.1 | async-start | bytes 524288 | tf_op jit(solution)/shard_map/all_to_all | solution.py:120
  60.4 12.6 %all-to-all-done.1 = bf16[128,8,128]{2,1,0:T(8,128)(2,1)S(1)} async-done(((bf16[128,8,128]{2,1,0:T(8,128)(2,1)}), bf16[128,8,128]{2,1,0:T(8,128)(2,1)S(1)}, u32[]{:S(2)}, u32[]{:S(2)}) %all-to-all-start.1) | async-done | bytes 262176 | tf_op jit(solution)/shard_map/all_to_all | solution.py:120
  73.7 187.1 %while.21 = (s32[]{:T(128)}, f32[128,512]{1,0:T(8,128)}, f32[9,8,128]{2,1,0:T(8,128)}, f32[8,128,128]{2,0,1:T(8,128)}, s32[4]{0:T(128)S(1)}, /*index=5*/s32[4]{0...) while((s32[]{:T(128)}, f32[128,512]{1,0:T(8,128)}, ...), condition=%wide.region_13.14_spmd.clone.clone, body=%wide.region_0.13_spmd.clone.clone.sunk | while | flops 448201472 | bytes 62394652 | solution.py:110
  82.8 1.4 gather_fusion
  89.3 2.2 exponential_multiply_fusion.2
  91.6 1.1 fusion.164
  93.2 1.2 convert_bitcast_fusion.2
  95.6 1.4 rsqrt_multiply_fusion.2
  97.1 1.8 fusion.171
  98.9 1.2 multiply_convert_fusion.2
  101.7 1.2 convolution_add_fusion.8
  105.5 1.5 copy.140
  107.0 3.4 fusion.167
  110.4 1.5 copy.141
  114.7 2.3 fusion.168
  128.7 1.4 gather_fusion
  135.2 2.2 exponential_multiply_fusion.2
  137.5 1.1 fusion.164
  139.1 1.2 convert_bitcast_fusion.2
  141.6 1.4 rsqrt_multiply_fusion.2
  143.1 1.8 fusion.171
  144.9 1.2 multiply_convert_fusion.2
  147.6 2.3 convolution_add_fusion.8
  152.6 1.5 copy.140
  154.0 3.4 fusion.167
  157.4 1.5 copy.141
  161.7 2.3 fusion.168
  175.7 1.4 gather_fusion
  182.3 2.2 exponential_multiply_fusion.2
  186.2 1.2 convert_bitcast_fusion.2
  188.6 1.5 rsqrt_multiply_fusion.2
  190.1 1.8 fusion.171
  191.9 1.2 multiply_convert_fusion.2
  194.7 2.3 convolution_add_fusion.8
  199.6 1.5 copy.140
  201.1 3.4 fusion.167
  204.4 1.5 copy.141
  208.8 2.3 fusion.168
  222.8 1.4 gather_fusion
  229.3 2.2 exponential_multiply_fusion.2
  233.2 1.2 convert_bitcast_fusion.2
  235.6 1.5 rsqrt_multiply_fusion.2
  237.1 1.8 fusion.171
  239.0 1.2 multiply_convert_fusion.2
  241.7 2.3 convolution_add_fusion.8
  246.6 1.5 copy.140
  248.1 3.4 fusion.167
  251.5 1.5 copy.141
  255.8 2.3 fusion.168
  260.8 1.9 copy.80
  262.7 6.5 %all-to-all-start.2 = ((f32[128,8,128]{2,1,0:T(8,128)}), f32[128,8,128]{2,1,0:T(8,128)S(1)}, u32[]{:S(2)}, u32[]{:S(2)}) async-start(f32[128,8,128]{2,1,0:T(8,128)} %bitcast.11), calls=%async_computation.2 | async-start | bytes 1048576 | tf_op jit(solution)/shard_map/all_to_all | solution.py:132
  270.0 19.5 %all-to-all-done.2 = f32[128,8,128]{2,1,0:T(8,128)S(1)} async-done(((f32[128,8,128]{2,1,0:T(8,128)}), f32[128,8,128]{2,1,0:T(8,128)S(1)}, u32[]{:S(2)}, u32[]{:S(2)}) %all-to-all-start.2) | async-done | bytes 524320 | tf_op jit(solution)/shard_map/all_to_all | solution.py:132
  289.5 4.0 scatter_custom_fusion
  295.4 6.4 %all-to-all-start.3 = ((f32[9,128,8]{0,2,1:T(8,128)}), f32[9,128,8]{0,2,1:T(8,128)S(1)}, u32[]{:S(2)}, u32[]{:S(2)}) async-start(f32[9,128,8]{0,2,1:T(8,128)} %bitcast.13), calls=%async_computation.3 | async-start | bytes 1048576 | tf_op jit(solution)/shard_map/all_to_all | solution.py:131
  301.7 20.4 %all-to-all-done.3 = f32[9,128,8]{0,2,1:T(8,128)S(1)} async-done(((f32[9,128,8]{0,2,1:T(8,128)}), f32[9,128,8]{0,2,1:T(8,128)S(1)}, u32[]{:S(2)}, u32[]{:S(2)}) %all-to-all-start.3) | async-done | bytes 36896 | tf_op jit(solution)/shard_map/all_to_all | solution.py:131
  322.2 3.4 scatter_custom_fusion.1
  326.4 222.5 %all-reduce.14.cloned.1.call-done = f32[128,512]{1,0:T(8,128)} async-done(((f32[128,512]{1,0:T(8,128)}), f32[128,512]{1,0:T(8,128)}) %all-reduce.14.cloned.1.call-update) | async-done | bytes 262160 | tf_op jit(solution)/shard_map/psum | solution.py:139
  548.8 1.7 broadcast_multiply_fusion.2
  550.5 51.4 %all-reduce.12.cloned.1.call-done = f32[1024,128]{1,0:T(8,128)} async-done(((f32[1024,128]{1,0:T(8,128)}), f32[1024,128]{1,0:T(8,128)}) %all-reduce.12.cloned.1.call-update) | async-done | bytes 524304 | tf_op jit(solution)/shard_map/psum | solution.py:136
  602.0 1.6 constant_dynamic-slice_fusion.1
  (485 shorter events, 96.0 us)
Async XLA Ops:
  7.2 24.3 %copy-start = (bf16[1024,128]{1,0:T(8,128)(2,1)S(1)}, bf16[1024,128]{1,0:T(8,128)(2,1)}, u32[]{:S(2)}) copy-start(bf16[1024,128]{1,0:T(8,128)(2,1)} %param.10) | copy-start | bytes 786436
  14.1 37.7 %all-to-all-start = ((f32[9,128,8]{0,2,1:T(8,128)}), f32[9,128,8]{0,2,1:T(8,128)S(1)}, u32[]{:S(2)}, u32[]{:S(2)}) async-start(f32[9,128,8]{0,2,1:T(8,128)} %bitcast_select_fusion.1), calls=%async_computation | async-start | bytes 1048576 | tf_op jit(solution)/shard_map/all_to_all | solution.py:118
  51.8 21.3 %all-to-all-start.1 = ((bf16[128,8,128]{2,1,0:T(8,128)(2,1)}), bf16[128,8,128]{2,1,0:T(8,128)(2,1)S(1)}, u32[]{:S(2)}, u32[]{:S(2)}) async-start(bf16[128,8,128]{2,1,0:T(8,128)(2,1)} %bitcast_select_fusion.2), calls=%async_computation.1 | async-start | bytes 524288 | tf_op jit(solution)/shard_map/all_to_all | solution.py:120
  73.7 13.7 %copy-start.8 = (bf16[8,128,128]{2,1,0:T(8,128)(2,1)}, bf16[8,128,128]{2,1,0:T(8,128)(2,1)S(1)}, u32[]{:S(2)}) copy-start(bf16[8,128,128]{2,1,0:T(8,128)(2,1)S(1)} %get-tuple-element.843) | copy-start | bytes 786436 | tf_op jit(solution)/shard_map/while
  81.3 22.9 %copy-start.21 = (f32[256]{0:T(256)}, f32[256]{0:T(256)S(1)}, u32[]{:S(2)}) copy-start(f32[256]{0:T(256)S(1)} %get-tuple-element.768) | copy-start | bytes 3076 | tf_op jit(solution)/shard_map/while
  81.3 22.9 %copy-start.23 = (f32[256]{0:T(256)}, f32[256]{0:T(256)S(1)}, u32[]{:S(2)}) copy-start(f32[256]{0:T(256)S(1)} %get-tuple-element.765) | copy-start | bytes 3076 | tf_op jit(solution)/shard_map/while
  82.0 19.6 %copy-start.28 = (s32[8]{0:T(128)}, s32[8]{0:T(128)S(1)}, u32[]{:S(2)}) copy-start(s32[8]{0:T(128)S(1)} %get-tuple-element.785) | copy-start | bytes 100 | tf_op jit(solution)/shard_map/while
  84.2 18.9 %copy-start.5 = (f32[9,8,128]{2,0,1:T(8,128)}, f32[9,8,128]{2,0,1:T(8,128)S(1)}, u32[]{:S(2)}) copy-start(f32[9,8,128]{2,0,1:T(8,128)S(1)} %select_bitcast_fusion.2) | copy-start | bytes 110596 | tf_op jit(solution)/shard_map/while
  84.9 19.4 %copy-start.11 = (f32[1,8,128]{2,0,1:T(1,128)}, f32[1,8,128]{2,0,1:T(1,128)S(1)}, u32[]{:S(2)}) copy-start(f32[1,8,128]{2,0,1:T(1,128)S(1)} %get-tuple-element.769) | copy-start | bytes 12292 | tf_op jit(solution)/shard_map/while
  85.5 18.8 %copy-start.16 = (f32[1024]{0:T(1024)}, f32[1024]{0:T(1024)S(1)}, u32[]{:S(2)}) copy-start(f32[1024]{0:T(1024)S(1)} %bitcast_multiply_fusion.8) | copy-start | bytes 12292 | tf_op jit(solution)/shard_map/while
  111.9 2.1 copy-start.3
  114.7 2.3 copy-start.15
  114.7 2.3 copy-start.26
  114.7 2.4 copy-start.27
  114.7 3.3 copy-start.25
  117.0 2.6 copy-start.9
  119.6 13.7 %copy-start.8 = (bf16[8,128,128]{2,1,0:T(8,128)(2,1)}, bf16[8,128,128]{2,1,0:T(8,128)(2,1)S(1)}, u32[]{:S(2)}) copy-start(bf16[8,128,128]{2,1,0:T(8,128)(2,1)S(1)} %get-tuple-element.843) | copy-start | bytes 786436 | tf_op jit(solution)/shard_map/while
  127.3 24.0 %copy-start.21 = (f32[256]{0:T(256)}, f32[256]{0:T(256)S(1)}, u32[]{:S(2)}) copy-start(f32[256]{0:T(256)S(1)} %get-tuple-element.768) | copy-start | bytes 3076 | tf_op jit(solution)/shard_map/while
  127.3 24.0 %copy-start.23 = (f32[256]{0:T(256)}, f32[256]{0:T(256)S(1)}, u32[]{:S(2)}) copy-start(f32[256]{0:T(256)S(1)} %get-tuple-element.765) | copy-start | bytes 3076 | tf_op jit(solution)/shard_map/while
  128.0 19.6 %copy-start.28 = (s32[8]{0:T(128)}, s32[8]{0:T(128)S(1)}, u32[]{:S(2)}) copy-start(s32[8]{0:T(128)S(1)} %get-tuple-element.785) | copy-start | bytes 100 | tf_op jit(solution)/shard_map/while
  130.2 20.0 %copy-start.5 = (f32[9,8,128]{2,0,1:T(8,128)}, f32[9,8,128]{2,0,1:T(8,128)S(1)}, u32[]{:S(2)}) copy-start(f32[9,8,128]{2,0,1:T(8,128)S(1)} %select_bitcast_fusion.2) | copy-start | bytes 110596 | tf_op jit(solution)/shard_map/while
  130.8 20.5 %copy-start.11 = (f32[1,8,128]{2,0,1:T(1,128)}, f32[1,8,128]{2,0,1:T(1,128)S(1)}, u32[]{:S(2)}) copy-start(f32[1,8,128]{2,0,1:T(1,128)S(1)} %get-tuple-element.769) | copy-start | bytes 12292 | tf_op jit(solution)/shard_map/while
  131.4 19.9 %copy-start.16 = (f32[1024]{0:T(1024)}, f32[1024]{0:T(1024)S(1)}, u32[]{:S(2)}) copy-start(f32[1024]{0:T(1024)S(1)} %bitcast_multiply_fusion.8) | copy-start | bytes 12292 | tf_op jit(solution)/shard_map/while
  147.3 2.6 copy-start.7
  147.6 2.3 copy-start.4
  161.7 2.3 copy-start.15
  161.7 2.3 copy-start.26
  161.7 2.4 copy-start.27
  161.7 3.3 copy-start.25
  164.0 2.6 copy-start.9
  166.6 13.7 %copy-start.8 = (bf16[8,128,128]{2,1,0:T(8,128)(2,1)}, bf16[8,128,128]{2,1,0:T(8,128)(2,1)S(1)}, u32[]{:S(2)}) copy-start(bf16[8,128,128]{2,1,0:T(8,128)(2,1)S(1)} %get-tuple-element.843) | copy-start | bytes 786436 | tf_op jit(solution)/shard_map/while
  174.3 24.0 %copy-start.21 = (f32[256]{0:T(256)}, f32[256]{0:T(256)S(1)}, u32[]{:S(2)}) copy-start(f32[256]{0:T(256)S(1)} %get-tuple-element.768) | copy-start | bytes 3076 | tf_op jit(solution)/shard_map/while
  174.3 24.0 %copy-start.23 = (f32[256]{0:T(256)}, f32[256]{0:T(256)S(1)}, u32[]{:S(2)}) copy-start(f32[256]{0:T(256)S(1)} %get-tuple-element.765) | copy-start | bytes 3076 | tf_op jit(solution)/shard_map/while
  175.0 19.6 %copy-start.28 = (s32[8]{0:T(128)}, s32[8]{0:T(128)S(1)}, u32[]{:S(2)}) copy-start(s32[8]{0:T(128)S(1)} %get-tuple-element.785) | copy-start | bytes 100 | tf_op jit(solution)/shard_map/while
  177.2 20.0 %copy-start.5 = (f32[9,8,128]{2,0,1:T(8,128)}, f32[9,8,128]{2,0,1:T(8,128)S(1)}, u32[]{:S(2)}) copy-start(f32[9,8,128]{2,0,1:T(8,128)S(1)} %select_bitcast_fusion.2) | copy-start | bytes 110596 | tf_op jit(solution)/shard_map/while
  177.8 20.5 %copy-start.11 = (f32[1,8,128]{2,0,1:T(1,128)}, f32[1,8,128]{2,0,1:T(1,128)S(1)}, u32[]{:S(2)}) copy-start(f32[1,8,128]{2,0,1:T(1,128)S(1)} %get-tuple-element.769) | copy-start | bytes 12292 | tf_op jit(solution)/shard_map/while
  178.4 19.9 %copy-start.16 = (f32[1024]{0:T(1024)}, f32[1024]{0:T(1024)S(1)}, u32[]{:S(2)}) copy-start(f32[1024]{0:T(1024)S(1)} %bitcast_multiply_fusion.8) | copy-start | bytes 12292 | tf_op jit(solution)/shard_map/while
  194.3 2.6 copy-start.7
  194.6 2.3 copy-start.4
  205.9 2.1 copy-start.3
  208.7 2.3 copy-start.15
  208.7 2.3 copy-start.26
  208.7 2.4 copy-start.27
  208.7 3.3 copy-start.25
  211.0 2.6 copy-start.9
  213.7 13.7 %copy-start.8 = (bf16[8,128,128]{2,1,0:T(8,128)(2,1)}, bf16[8,128,128]{2,1,0:T(8,128)(2,1)S(1)}, u32[]{:S(2)}) copy-start(bf16[8,128,128]{2,1,0:T(8,128)(2,1)S(1)} %get-tuple-element.843) | copy-start | bytes 786436 | tf_op jit(solution)/shard_map/while
  221.3 24.0 %copy-start.21 = (f32[256]{0:T(256)}, f32[256]{0:T(256)S(1)}, u32[]{:S(2)}) copy-start(f32[256]{0:T(256)S(1)} %get-tuple-element.768) | copy-start | bytes 3076 | tf_op jit(solution)/shard_map/while
  221.3 24.0 %copy-start.23 = (f32[256]{0:T(256)}, f32[256]{0:T(256)S(1)}, u32[]{:S(2)}) copy-start(f32[256]{0:T(256)S(1)} %get-tuple-element.765) | copy-start | bytes 3076 | tf_op jit(solution)/shard_map/while
  222.0 19.6 %copy-start.28 = (s32[8]{0:T(128)}, s32[8]{0:T(128)S(1)}, u32[]{:S(2)}) copy-start(s32[8]{0:T(128)S(1)} %get-tuple-element.785) | copy-start | bytes 100 | tf_op jit(solution)/shard_map/while
  224.2 20.0 %copy-start.5 = (f32[9,8,128]{2,0,1:T(8,128)}, f32[9,8,128]{2,0,1:T(8,128)S(1)}, u32[]{:S(2)}) copy-start(f32[9,8,128]{2,0,1:T(8,128)S(1)} %select_bitcast_fusion.2) | copy-start | bytes 110596 | tf_op jit(solution)/shard_map/while
  224.9 20.5 %copy-start.11 = (f32[1,8,128]{2,0,1:T(1,128)}, f32[1,8,128]{2,0,1:T(1,128)S(1)}, u32[]{:S(2)}) copy-start(f32[1,8,128]{2,0,1:T(1,128)S(1)} %get-tuple-element.769) | copy-start | bytes 12292 | tf_op jit(solution)/shard_map/while
  225.5 19.9 %copy-start.16 = (f32[1024]{0:T(1024)}, f32[1024]{0:T(1024)S(1)}, u32[]{:S(2)}) copy-start(f32[1024]{0:T(1024)S(1)} %bitcast_multiply_fusion.8) | copy-start | bytes 12292 | tf_op jit(solution)/shard_map/while
  241.4 2.6 copy-start.7
  241.7 2.3 copy-start.4
  253.0 2.1 copy-start.3
  255.8 2.3 copy-start.15
  255.8 2.3 copy-start.26
  255.8 2.4 copy-start.27
  255.8 3.3 copy-start.25
  258.1 2.6 copy-start.9
  262.7 26.8 %all-to-all-start.2 = ((f32[128,8,128]{2,1,0:T(8,128)}), f32[128,8,128]{2,1,0:T(8,128)S(1)}, u32[]{:S(2)}, u32[]{:S(2)}) async-start(f32[128,8,128]{2,1,0:T(8,128)} %bitcast.11), calls=%async_computation.2 | async-start | bytes 1048576 | tf_op jit(solution)/shard_map/all_to_all | solution.py:132
  269.2 279.6 %all-reduce.14.cloned.1.call-start = ((), (), s32[]{:S(2)}) async-start(), calls=%async_computation.5 | async-start | bytes 524288 | tf_op jit(solution)/shard_map/psum | solution.py:139
  269.9 332.0 %all-reduce.12.cloned.1.call-start = ((), (), s32[]{:S(2)}) async-start(), calls=%async_computation.4 | async-start | bytes 1048576 | tf_op jit(solution)/shard_map/psum | solution.py:136
  295.4 26.8 %all-to-all-start.3 = ((f32[9,128,8]{0,2,1:T(8,128)}), f32[9,128,8]{0,2,1:T(8,128)S(1)}, u32[]{:S(2)}, u32[]{:S(2)}) async-start(f32[9,128,8]{0,2,1:T(8,128)} %bitcast.13), calls=%async_computation.3 | async-start | bytes 1048576 | tf_op jit(solution)/shard_map/all_to_all | solution.py:131
  (73 other events, 68.1 us)
Sparse Core Ops, SparseCore 0:
  275.6 273.1 all-reduce.13
  551.3 50.6 all-reduce.11
where the time goes:
time: 613 us; the launch traced here: 610 us
  waiting for transfers between devices  343 us (56%)
  local copies, waits for them, and re-layouts  79.9 us (13%)
  other arithmetic  76.6 us (12%)
  matrix products  39.1 us (6%)
  starting transfers between devices  36.8 us (6%)
  loops' own time  20.3 us (3%)
  between operations  14.3 us (2%)
    psum x1, waiting for transfers between devices, on_device(): lax.psum(decoder_sum, ('gs', 'view')) * (1.0 / math.sqrt(pixel_total))  222 us
    psum x1, waiting for transfers between devices, on_device(): summed = lax.psum(feat_own, 'view')  51.4 us
    another operation x8, other arithmetic, composite(): inner = jnp.cumsum(blocked, axis=2) - blocked  22.4 us
    all_to_all x1, waiting for transfers between devices, on_device(): lax.all_to_all(geo_acc, 'gs', split_axis=1, concat_axis=1, tiled=True)  20.4 us
    another operation x1, loops' own time, device_terms(): lax.scan(tile_step, start_totals, tile_range)  20.3 us
    all_to_all x1, waiting for transfers between devices, on_device(): lax.all_to_all(feat_acc, 'gs', split_axis=0, concat_axis=0, tiled=True)  19.5 us
    while x264, local copies, waits for them, and re-layouts  19.3 us
    all_to_all x1, starting transfers between devices, on_device(): lax.all_to_all(geo_send, 'gs', split_axis=1, concat_axis=1, tiled=True)  17.4 us
  transfers between devices with their start and end apart: 6, of which 6 were waited for; matrix products, arithmetic and copies ran while one was open for 3% of the time, Pallas kernels for 0%

commit v1 on v0

--- a/solution.py
+++ b/solution.py
@@ -128,7 +128,17 @@
         tile_lengths[0],
         shard_index,
     )
-    returned_geo = lax.all_to_all(geo_acc, "gs", split_axis=1, concat_axis=1, tiled=True)
+
+    def view_the_tasks(vals):
+        all_rows = jnp.concatenate(
+            jax.lax.all_to_all(
+                jnp.stack(jnp.split(vals, jax.lax.axis_size("gs"), 1), 0), "gs", 0, 0
+            ),
+            1,
+        )
+        return all_rows
+
+    returned_geo = view_the_tasks(geo_acc)
     returned_feat = lax.all_to_all(feat_acc, "gs", split_axis=0, concat_axis=0, tiled=True)
     geo_own = jnp.zeros_like(returned_geo).at[:, send_order].set(returned_geo)
     feat_own = jnp.zeros_like(returned_feat).at[send_order].set(returned_feat)

time: 613 us -> 589 us (0.961)
  waiting for transfers between devices: 343 us -> 241 us
  local copies, waits for them, and re-layouts: 79.9 us -> 150 us
  starting transfers between devices: 36.8 us -> 44.2 us
    psum x1, waiting for transfers between devices: 222 us -> 140 us  [on_device(): lax.psum(decoder_sum, ('gs', 'view')) * (1.0 / math.sqrt(pixel_total))]
    unnamed x19 -> x146, local copies, waits for them, and re-layouts: 5.75 us -> 79.4 us
    all_to_all x1, waiting for transfers between devices: 19.5 us -> 0.01 us  [on_device(): lax.all_to_all(feat_acc, 'gs', split_axis=0, concat_axis=0, tiled=True)]
    all_to_all x1, starting transfers between devices: 6.36 us -> 13.7 us  [view_the_tasks(): jax.lax.all_to_all(jnp.stack(jnp.split(vals, jax.lax.axis_size('gs'), 1),...]
    while x264 -> x280, local copies, waits for them, and re-layouts: 19.3 us -> 19.2 us
  transfers between devices with their start and end apart: 6 -> 6, of which waited for: 6 -> 5; matrix products, arithmetic and copies ran while one was open for 3% -> 15% of each run, Pallas kernels for 0% -> 0%
where the time goes in v1:
time: 589 us; the launch traced here: 586 us
  waiting for transfers between devices  241 us (41%)
  local copies, waits for them, and re-layouts  150 us (25%)
  other arithmetic  76.6 us (13%)
  starting transfers between devices  44.2 us (8%)
  matrix products  39.2 us (7%)
  loops' own time  20.6 us (3%)
  between operations  14.4 us (2%)
    psum x1, waiting for transfers between devices, on_device(): lax.psum(decoder_sum, ('gs', 'view')) * (1.0 / math.sqrt(pixel_total))  140 us
    unnamed x146, local copies, waits for them, and re-layouts  79.4 us
    psum x1, waiting for transfers between devices, on_device(): summed = lax.psum(feat_own, 'view')  51.4 us
    another operation x8, other arithmetic, composite(): inner = jnp.cumsum(blocked, axis=2) - blocked  22.4 us
    another operation x1, loops' own time, device_terms(): lax.scan(tile_step, start_totals, tile_range)  20.6 us
    all_to_all x1, waiting for transfers between devices, view_the_tasks(): jax.lax.all_to_all(jnp.stack(jnp.split(vals, jax.lax.axis_size('gs'), 1),...  20.4 us
    while x280, local copies, waits for them, and re-layouts  19.2 us
    all_to_all x1, starting transfers between devices, on_device(): lax.all_to_all(geo_send, 'gs', split_axis=1, concat_axis=1, tiled=True)  17.4 us
  transfers between devices with their start and end apart: 6, of which 5 were waited for; matrix products, arithmetic and copies ran while one was open for 15% of the time, Pallas kernels for 0%

profile of v1, /device:TPU:8, one launch (start us, length us, event | category | flops | bytes accessed | tf_op | source)
XLA Modules:
  0.0 586.3 jit_solution(11409221392307989041)
XLA Ops:
  10.2 2.8 gather_fusion.2
  14.1 17.4 %all-to-all-start = ((f32[9,128,8]{0,2,1:T(8,128)}), f32[9,128,8]{0,2,1:T(8,128)S(1)}, u32[]{:S(2)}, u32[]{:S(2)}) async-start(f32[9,128,8]{0,2,1:T(8,128)} %bitcast_select_fusion.1), calls=%async_computation | async-start | bytes 1048576 | tf_op jit(solution)/shard_map/all_to_all | solution.py:118
  31.4 3.2 gather_fusion.3
  35.6 16.2 %all-to-all-done = f32[9,128,8]{0,2,1:T(8,128)S(1)} async-done(((f32[9,128,8]{0,2,1:T(8,128)}), f32[9,128,8]{0,2,1:T(8,128)S(1)}, u32[]{:S(2)}, u32[]{:S(2)}) %all-to-all-start) | async-done | bytes 36896 | tf_op jit(solution)/shard_map/all_to_all | solution.py:118
  51.7 6.5 %all-to-all-start.1 = ((bf16[128,8,128]{2,1,0:T(8,128)(2,1)}), bf16[128,8,128]{2,1,0:T(8,128)(2,1)S(1)}, u32[]{:S(2)}, u32[]{:S(2)}) async-start(bf16[128,8,128]{2,1,0:T(8,128)(2,1)} %bitcast_select_fusion.2), calls=%async_computation.1 | async-start | bytes 524288 | tf_op jit(solution)/shard_map/all_to_all | solution.py:120
  59.8 13.2 %all-to-all-done.1 = bf16[128,8,128]{2,1,0:T(8,128)(2,1)S(1)} async-done(((bf16[128,8,128]{2,1,0:T(8,128)(2,1)}), bf16[128,8,128]{2,1,0:T(8,128)(2,1)S(1)}, u32[]{:S(2)}, u32[]{:S(2)}) %all-to-all-start.1) | async-done | bytes 262176 | tf_op jit(solution)/shard_map/all_to_all | solution.py:120
  73.6 184.3 %while.21 = (s32[]{:T(128)}, f32[128,512]{1,0:T(8,128)}, f32[9,8,128]{2,1,0:T(8,128)}, f32[8,128,128]{2,0,1:T(8,128)}, s32[4]{0:T(128)S(1)}, /*index=5*/s32[4]{0...) while((s32[]{:T(128)}, f32[128,512]{1,0:T(8,128)}, ...), condition=%wide.region_13.14_spmd.clone.clone, body=%wide.region_0.13_spmd.clone.clone.sunk | while | flops 448201472 | bytes 62689620 | solution.py:110
  88.5 2.2 exponential_multiply_fusion.2
  90.8 1.1 fusion.164
  92.4 1.2 convert_bitcast_fusion.2
  94.9 1.4 rsqrt_multiply_fusion.2
  96.3 1.8 fusion.171
  98.2 1.2 multiply_convert_fusion.2
  100.9 1.2 convolution_add_fusion.8
  102.4 1.1 convolution_add_fusion.7
  104.8 1.5 copy.716
  106.3 3.4 fusion.167
  109.6 1.5 copy.717
  113.9 2.3 fusion.168
  133.7 2.2 exponential_multiply_fusion.2
  136.0 1.1 fusion.164
  137.6 1.2 convert_bitcast_fusion.2
  140.1 1.4 rsqrt_multiply_fusion.2
  141.5 1.8 fusion.171
  143.4 1.2 multiply_convert_fusion.2
  146.1 2.3 convolution_add_fusion.8
  148.7 1.1 convolution_add_fusion.7
  151.1 1.5 copy.716
  152.6 3.4 fusion.167
  155.9 1.5 copy.717
  160.2 2.3 fusion.168
  180.0 2.2 exponential_multiply_fusion.2
  182.3 1.1 fusion.164
  183.9 1.2 convert_bitcast_fusion.2
  186.3 1.5 rsqrt_multiply_fusion.2
  187.8 1.8 fusion.171
  189.7 1.2 multiply_convert_fusion.2
  192.4 2.3 convolution_add_fusion.8
  197.4 1.5 copy.716
  198.9 3.4 fusion.167
  202.2 1.5 copy.717
  206.5 2.3 fusion.168
  226.3 2.2 exponential_multiply_fusion.2
  228.6 1.1 fusion.164
  230.2 1.2 convert_bitcast_fusion.2
  232.6 1.5 rsqrt_multiply_fusion.2
  234.1 1.8 fusion.171
  236.0 1.2 multiply_convert_fusion.2
  238.7 2.3 convolution_add_fusion.8
  241.3 1.1 convolution_add_fusion.7
  243.7 1.5 copy.716
  245.1 3.4 fusion.167
  248.5 1.5 copy.717
  252.8 2.3 fusion.168
  257.9 1.9 copy.657
  259.9 6.5 %all-to-all-start.2 = ((f32[128,8,128]{2,1,0:T(8,128)}), f32[128,8,128]{2,1,0:T(8,128)S(1)}, u32[]{:S(2)}, u32[]{:S(2)}) async-start(f32[128,8,128]{2,1,0:T(8,128)} %bitcast.11), calls=%async_computation.2 | async-start | bytes 1048576 | tf_op jit(solution)/shard_map/all_to_all | solution.py:142
  341.8 4.0 scatter_custom_fusion
  346.4 13.7 %all-to-all-start.3 = ((f32[128,9,8]{1,2,0:T(8,128)}), f32[128,9,8]{1,2,0:T(8,128)S(1)}, u32[]{:S(2)}, u32[]{:S(2)}) async-start(f32[128,9,8]{1,2,0:T(8,128)} %constant_dynamic-update-slice_fusion), calls=%async_computation.3 | async-start | bytes 1048576 | tf_op jit(solution)/shard_map/all_to_all | solution.py:134
  360.2 20.4 %all-to-all-done.3 = f32[128,9,8]{1,2,0:T(8,128)S(1)} async-done(((f32[128,9,8]{1,2,0:T(8,128)}), f32[128,9,8]{1,2,0:T(8,128)S(1)}, u32[]{:S(2)}, u32[]{:S(2)}) %all-to-all-start.3) | async-done | bytes 36896 | tf_op jit(solution)/shard_map/all_to_all | solution.py:134
  380.5 3.4 scatter_custom_fusion.1
  384.7 140.1 %all-reduce.14.cloned.1.call-done = f32[128,512]{1,0:T(8,128)} async-done(((f32[128,512]{1,0:T(8,128)}), f32[128,512]{1,0:T(8,128)}) %all-reduce.14.cloned.1.call-update) | async-done | bytes 262160 | tf_op jit(solution)/shard_map/psum | solution.py:149
  524.8 1.7 broadcast_multiply_fusion.2
  526.5 51.4 %all-reduce.12.cloned.1.call-done = f32[1024,128]{1,0:T(8,128)} async-done(((f32[1024,128]{1,0:T(8,128)}), f32[1024,128]{1,0:T(8,128)}) %all-reduce.12.cloned.1.call-update) | async-done | bytes 524304 | tf_op jit(solution)/shard_map/psum | solution.py:146
  577.9 1.6 constant_dynamic-slice_fusion.1
  (629 shorter events, 165.7 us)
Async XLA Ops:
  7.2 24.3 %copy-start = (bf16[1024,128]{1,0:T(8,128)(2,1)S(1)}, bf16[1024,128]{1,0:T(8,128)(2,1)}, u32[]{:S(2)}) copy-start(bf16[1024,128]{1,0:T(8,128)(2,1)} %param.10) | copy-start | bytes 786436
  14.1 37.7 %all-to-all-start = ((f32[9,128,8]{0,2,1:T(8,128)}), f32[9,128,8]{0,2,1:T(8,128)S(1)}, u32[]{:S(2)}, u32[]{:S(2)}) async-start(f32[9,128,8]{0,2,1:T(8,128)} %bitcast_select_fusion.1), calls=%async_computation | async-start | bytes 1048576 | tf_op jit(solution)/shard_map/all_to_all | solution.py:118
  51.7 21.2 %all-to-all-start.1 = ((bf16[128,8,128]{2,1,0:T(8,128)(2,1)}), bf16[128,8,128]{2,1,0:T(8,128)(2,1)S(1)}, u32[]{:S(2)}, u32[]{:S(2)}) async-start(bf16[128,8,128]{2,1,0:T(8,128)(2,1)} %bitcast_select_fusion.2), calls=%async_computation.1 | async-start | bytes 524288 | tf_op jit(solution)/shard_map/all_to_all | solution.py:120
  58.2 466.6 %all-reduce.14.cloned.1.call-start = ((), (), s32[]{:S(2)}) async-start(), calls=%async_computation.5 | async-start | bytes 524288 | tf_op jit(solution)/shard_map/psum | solution.py:149
  73.7 10.4 %copy-start.21 = (f32[9,8,128]{2,0,1:T(8,128)}, f32[9,8,128]{2,0,1:T(8,128)S(1)}, u32[]{:S(2)}) copy-start(f32[9,8,128]{2,0,1:T(8,128)S(1)} %get-tuple-element.891) | copy-start | bytes 110596 | tf_op jit(solution)/shard_map/while
  73.7 12.9 %copy-start.8 = (bf16[8,128,128]{2,1,0:T(8,128)(2,1)}, bf16[8,128,128]{2,1,0:T(8,128)(2,1)S(1)}, u32[]{:S(2)}) copy-start(bf16[8,128,128]{2,1,0:T(8,128)(2,1)S(1)} %get-tuple-element.894) | copy-start | bytes 786436 | tf_op jit(solution)/shard_map/while
  81.4 22.1 %copy-start.23 = (f32[256]{0:T(256)}, f32[256]{0:T(256)S(1)}, u32[]{:S(2)}) copy-start(f32[256]{0:T(256)S(1)} %get-tuple-element.819) | copy-start | bytes 3076 | tf_op jit(solution)/shard_map/while
  81.4 22.1 %copy-start.25 = (f32[256]{0:T(256)}, f32[256]{0:T(256)S(1)}, u32[]{:S(2)}) copy-start(f32[256]{0:T(256)S(1)} %get-tuple-element.816) | copy-start | bytes 3076 | tf_op jit(solution)/shard_map/while
  82.1 18.8 %copy-start.30 = (s32[8]{0:T(128)}, s32[8]{0:T(128)S(1)}, u32[]{:S(2)}) copy-start(s32[8]{0:T(128)S(1)} %get-tuple-element.836) | copy-start | bytes 100 | tf_op jit(solution)/shard_map/while
  83.4 19.0 %copy-start.5 = (f32[9,8,128]{2,0,1:T(8,128)}, f32[9,8,128]{2,0,1:T(8,128)S(1)}, u32[]{:S(2)}) copy-start(f32[9,8,128]{2,0,1:T(8,128)S(1)} %select_bitcast_fusion.2) | copy-start | bytes 110596 | tf_op jit(solution)/shard_map/while
  84.1 19.4 %copy-start.11 = (f32[1,8,128]{2,0,1:T(1,128)}, f32[1,8,128]{2,0,1:T(1,128)S(1)}, u32[]{:S(2)}) copy-start(f32[1,8,128]{2,0,1:T(1,128)S(1)} %get-tuple-element.820) | copy-start | bytes 12292 | tf_op jit(solution)/shard_map/while
  84.7 18.9 %copy-start.16 = (f32[1024]{0:T(1024)}, f32[1024]{0:T(1024)S(1)}, u32[]{:S(2)}) copy-start(f32[1024]{0:T(1024)S(1)} %bitcast_multiply_fusion.8) | copy-start | bytes 12292 | tf_op jit(solution)/shard_map/while
  113.9 2.3 copy-start.15
  113.9 2.3 copy-start.28
  113.9 2.4 copy-start.29
  113.9 3.3 copy-start.27
  116.2 2.6 copy-start.9
  118.8 10.4 %copy-start.21 = (f32[9,8,128]{2,0,1:T(8,128)}, f32[9,8,128]{2,0,1:T(8,128)S(1)}, u32[]{:S(2)}) copy-start(f32[9,8,128]{2,0,1:T(8,128)S(1)} %get-tuple-element.891) | copy-start | bytes 110596 | tf_op jit(solution)/shard_map/while
  118.9 12.9 %copy-start.8 = (bf16[8,128,128]{2,1,0:T(8,128)(2,1)}, bf16[8,128,128]{2,1,0:T(8,128)(2,1)S(1)}, u32[]{:S(2)}) copy-start(bf16[8,128,128]{2,1,0:T(8,128)(2,1)S(1)} %get-tuple-element.894) | copy-start | bytes 786436 | tf_op jit(solution)/shard_map/while
  126.5 23.2 %copy-start.23 = (f32[256]{0:T(256)}, f32[256]{0:T(256)S(1)}, u32[]{:S(2)}) copy-start(f32[256]{0:T(256)S(1)} %get-tuple-element.819) | copy-start | bytes 3076 | tf_op jit(solution)/shard_map/while
  126.6 23.2 %copy-start.25 = (f32[256]{0:T(256)}, f32[256]{0:T(256)S(1)}, u32[]{:S(2)}) copy-start(f32[256]{0:T(256)S(1)} %get-tuple-element.816) | copy-start | bytes 3076 | tf_op jit(solution)/shard_map/while
  127.3 18.8 %copy-start.30 = (s32[8]{0:T(128)}, s32[8]{0:T(128)S(1)}, u32[]{:S(2)}) copy-start(s32[8]{0:T(128)S(1)} %get-tuple-element.836) | copy-start | bytes 100 | tf_op jit(solution)/shard_map/while
  128.6 20.1 %copy-start.5 = (f32[9,8,128]{2,0,1:T(8,128)}, f32[9,8,128]{2,0,1:T(8,128)S(1)}, u32[]{:S(2)}) copy-start(f32[9,8,128]{2,0,1:T(8,128)S(1)} %select_bitcast_fusion.2) | copy-start | bytes 110596 | tf_op jit(solution)/shard_map/while
  129.3 20.5 %copy-start.11 = (f32[1,8,128]{2,0,1:T(1,128)}, f32[1,8,128]{2,0,1:T(1,128)S(1)}, u32[]{:S(2)}) copy-start(f32[1,8,128]{2,0,1:T(1,128)S(1)} %get-tuple-element.820) | copy-start | bytes 12292 | tf_op jit(solution)/shard_map/while
  129.9 20.0 %copy-start.16 = (f32[1024]{0:T(1024)}, f32[1024]{0:T(1024)S(1)}, u32[]{:S(2)}) copy-start(f32[1024]{0:T(1024)S(1)} %bitcast_multiply_fusion.8) | copy-start | bytes 12292 | tf_op jit(solution)/shard_map/while
  145.8 2.6 copy-start.7
  146.1 2.3 copy-start.4
  160.2 2.3 copy-start.15
  160.2 2.3 copy-start.28
  160.2 2.4 copy-start.29
  160.2 3.3 copy-start.27
  162.5 2.6 copy-start.9
  165.1 10.4 %copy-start.21 = (f32[9,8,128]{2,0,1:T(8,128)}, f32[9,8,128]{2,0,1:T(8,128)S(1)}, u32[]{:S(2)}) copy-start(f32[9,8,128]{2,0,1:T(8,128)S(1)} %get-tuple-element.891) | copy-start | bytes 110596 | tf_op jit(solution)/shard_map/while
  165.1 12.9 %copy-start.8 = (bf16[8,128,128]{2,1,0:T(8,128)(2,1)}, bf16[8,128,128]{2,1,0:T(8,128)(2,1)S(1)}, u32[]{:S(2)}) copy-start(bf16[8,128,128]{2,1,0:T(8,128)(2,1)S(1)} %get-tuple-element.894) | copy-start | bytes 786436 | tf_op jit(solution)/shard_map/while
  172.8 23.2 %copy-start.23 = (f32[256]{0:T(256)}, f32[256]{0:T(256)S(1)}, u32[]{:S(2)}) copy-start(f32[256]{0:T(256)S(1)} %get-tuple-element.819) | copy-start | bytes 3076 | tf_op jit(solution)/shard_map/while
  172.8 23.2 %copy-start.25 = (f32[256]{0:T(256)}, f32[256]{0:T(256)S(1)}, u32[]{:S(2)}) copy-start(f32[256]{0:T(256)S(1)} %get-tuple-element.816) | copy-start | bytes 3076 | tf_op jit(solution)/shard_map/while
  173.5 18.8 %copy-start.30 = (s32[8]{0:T(128)}, s32[8]{0:T(128)S(1)}, u32[]{:S(2)}) copy-start(s32[8]{0:T(128)S(1)} %get-tuple-element.836) | copy-start | bytes 100 | tf_op jit(solution)/shard_map/while
  174.9 20.1 %copy-start.5 = (f32[9,8,128]{2,0,1:T(8,128)}, f32[9,8,128]{2,0,1:T(8,128)S(1)}, u32[]{:S(2)}) copy-start(f32[9,8,128]{2,0,1:T(8,128)S(1)} %select_bitcast_fusion.2) | copy-start | bytes 110596 | tf_op jit(solution)/shard_map/while
  175.6 20.5 %copy-start.11 = (f32[1,8,128]{2,0,1:T(1,128)}, f32[1,8,128]{2,0,1:T(1,128)S(1)}, u32[]{:S(2)}) copy-start(f32[1,8,128]{2,0,1:T(1,128)S(1)} %get-tuple-element.820) | copy-start | bytes 12292 | tf_op jit(solution)/shard_map/while
  176.2 20.0 %copy-start.16 = (f32[1024]{0:T(1024)}, f32[1024]{0:T(1024)S(1)}, u32[]{:S(2)}) copy-start(f32[1024]{0:T(1024)S(1)} %bitcast_multiply_fusion.8) | copy-start | bytes 12292 | tf_op jit(solution)/shard_map/while
  192.1 2.6 copy-start.7
  192.4 2.3 copy-start.4
  206.5 2.3 copy-start.28
  206.5 2.4 copy-start.29
  206.5 3.3 copy-start.27
  208.8 2.6 copy-start.9
  211.4 10.4 %copy-start.21 = (f32[9,8,128]{2,0,1:T(8,128)}, f32[9,8,128]{2,0,1:T(8,128)S(1)}, u32[]{:S(2)}) copy-start(f32[9,8,128]{2,0,1:T(8,128)S(1)} %get-tuple-element.891) | copy-start | bytes 110596 | tf_op jit(solution)/shard_map/while
  211.4 12.9 %copy-start.8 = (bf16[8,128,128]{2,1,0:T(8,128)(2,1)}, bf16[8,128,128]{2,1,0:T(8,128)(2,1)S(1)}, u32[]{:S(2)}) copy-start(bf16[8,128,128]{2,1,0:T(8,128)(2,1)S(1)} %get-tuple-element.894) | copy-start | bytes 786436 | tf_op jit(solution)/shard_map/while
  219.1 23.2 %copy-start.23 = (f32[256]{0:T(256)}, f32[256]{0:T(256)S(1)}, u32[]{:S(2)}) copy-start(f32[256]{0:T(256)S(1)} %get-tuple-element.819) | copy-start | bytes 3076 | tf_op jit(solution)/shard_map/while
  219.1 23.3 %copy-start.25 = (f32[256]{0:T(256)}, f32[256]{0:T(256)S(1)}, u32[]{:S(2)}) copy-start(f32[256]{0:T(256)S(1)} %get-tuple-element.816) | copy-start | bytes 3076 | tf_op jit(solution)/shard_map/while
  219.8 18.8 %copy-start.30 = (s32[8]{0:T(128)}, s32[8]{0:T(128)S(1)}, u32[]{:S(2)}) copy-start(s32[8]{0:T(128)S(1)} %get-tuple-element.836) | copy-start | bytes 100 | tf_op jit(solution)/shard_map/while
  221.2 20.1 %copy-start.5 = (f32[9,8,128]{2,0,1:T(8,128)}, f32[9,8,128]{2,0,1:T(8,128)S(1)}, u32[]{:S(2)}) copy-start(f32[9,8,128]{2,0,1:T(8,128)S(1)} %select_bitcast_fusion.2) | copy-start | bytes 110596 | tf_op jit(solution)/shard_map/while
  221.9 20.5 %copy-start.11 = (f32[1,8,128]{2,0,1:T(1,128)}, f32[1,8,128]{2,0,1:T(1,128)S(1)}, u32[]{:S(2)}) copy-start(f32[1,8,128]{2,0,1:T(1,128)S(1)} %get-tuple-element.820) | copy-start | bytes 12292 | tf_op jit(solution)/shard_map/while
  222.4 20.0 %copy-start.16 = (f32[1024]{0:T(1024)}, f32[1024]{0:T(1024)S(1)}, u32[]{:S(2)}) copy-start(f32[1024]{0:T(1024)S(1)} %bitcast_multiply_fusion.8) | copy-start | bytes 12292 | tf_op jit(solution)/shard_map/while
  238.4 2.6 copy-start.7
  238.7 2.3 copy-start.4
  252.8 2.3 copy-start.28
  252.8 2.4 copy-start.29
  252.8 3.3 copy-start.27
  255.1 2.6 copy-start.9
  259.9 6.6 %copy-start.20 = (f32[9,8,128]{2,1,0:T(8,128)S(1)}, f32[9,8,128]{2,1,0:T(8,128)}, u32[]{:S(2)}) copy-start(f32[9,8,128]{2,1,0:T(8,128)} %get-tuple-element.921) | copy-start | bytes 110596
  259.9 81.9 %all-to-all-start.2 = ((f32[128,8,128]{2,1,0:T(8,128)}), f32[128,8,128]{2,1,0:T(8,128)S(1)}, u32[]{:S(2)}, u32[]{:S(2)}) async-start(f32[128,8,128]{2,1,0:T(8,128)} %bitcast.11), calls=%async_computation.2 | async-start | bytes 1048576 | tf_op jit(solution)/shard_map/all_to_all | solution.py:142
  266.4 311.5 %all-reduce.12.cloned.1.call-start = ((), (), s32[]{:S(2)}) async-start(), calls=%async_computation.4 | async-start | bytes 1048576 | tf_op jit(solution)/shard_map/psum | solution.py:146
  346.4 34.1 %all-to-all-start.3 = ((f32[128,9,8]{1,2,0:T(8,128)}), f32[128,9,8]{1,2,0:T(8,128)S(1)}, u32[]{:S(2)}, u32[]{:S(2)}) async-start(f32[128,9,8]{1,2,0:T(8,128)} %constant_dynamic-update-slice_fusion), calls=%async_computation.3 | async-start | bytes 1048576 | tf_op jit(solution)/shard_map/all_to_all | solution.py:134
  (81 other events, 84.6 us)
Sparse Core Ops, SparseCore 0:
  260.0 264.7 all-reduce.13
  527.2 50.6 all-reduce.11
